TPU v7x, 32 devices: a whole 2x2x4 slice. The times are simulated.
32 devices in a mesh: grp: 2 (over y), rows: 8 (over z, x), mod: 2 (over core).
Axes of the slice: x: 2, y: 2, z: 4, core: 2. Of those that a mesh axis runs over, the one named last changes fastest.
Arguments:
- queries: bfloat16 [16, 8, 2304], P(('grp', 'rows'), 'mod'), parts along dimension 0, may hold values from -6 to 6
- train_grads: bfloat16 [2048, 8, 2304], P(('grp', 'rows'), 'mod'), parts along dimension 0, may hold values from -6 to 6
- factors: float32 [8, 2, 48, 48], P('mod'), may hold values from -4 to 4, as said below
Outputs:
- scores: float32 [16, 1024], P(('grp', 'mod'), 'rows'), parts along dimension 0
There are 2 independent parts, one for each index of `grp`. A program takes and returns all parts, laid end to end along the dimension named above; an argument that names none is the same for every part. Nothing has to cross between parts.
Inputs may be any that keep to these rules, and one draw needn't show every extreme that they name: `factors`: each factor is a 48 x 48 matrix with a positive diagonal and full rank.
All inputs are finite; a program needn't handle non-finite values.
Results may differ from a plain program's by a relative error of at most 0.0029.
Values may be sent and summed in bfloat16 or wider, within the bound.
No kernel may reach another device: no remote copies, remote signals or barrier semaphores. Data moves between devices by JAX's collectives and lax.ppermute only.
A program may use at most 64 MiB of HBM per device.

v0:
```python
import jax
import jax.numpy as jnp
from jax import lax
from jax.sharding import PartitionSpec as P

MODULES = 8
PROJ = 48
COORDS = 2304


def precondition(grads_in, factors):
    count = grads_in.shape[0]
    local_modules = grads_in.shape[1]
    grads = grads_in.astype(jnp.float32).reshape(count, local_modules, PROJ, PROJ)
    left_side = jnp.einsum("mab,qmbc->qmac", factors[:, 0], grads, precision=lax.Precision.HIGHEST)
    both_sides = jnp.einsum(
        "qmac,mcd->qmad", left_side, factors[:, 1], precision=lax.Precision.HIGHEST
    )
    both_sides = both_sides / jnp.sqrt(jnp.float32(MODULES * COORDS))
    return both_sides.astype(jnp.bfloat16).reshape(count, local_modules, PROJ * PROJ)


def shards(queries, train_grads, factors):
    train_count = train_grads.shape[0]
    train_flat = train_grads.reshape(train_count, -1)
    scaled_own = precondition(queries, factors)
    ready_rows = lax.all_gather(scaled_own, "rows", axis=0, tiled=True)
    flat_rows = ready_rows.reshape(ready_rows.shape[0], -1)
    partial_value = lax.dot_general(
        flat_rows, train_flat, (((1,), (1,)), ((), ())), preferred_element_type=jnp.float32
    )
    return lax.psum_scatter(partial_value, "mod", scatter_dimension=0, tiled=True)


def solution(mesh):
    in_specs = (
        P(("grp", "rows"), "mod", None),
        P(("grp", "rows"), "mod", None),
        P("mod", None, None, None),
    )
    out_specs = P(("grp", "mod"), "rows")
    return jax.shard_map(shards, mesh=mesh, in_specs=in_specs, out_specs=out_specs, check_vma=False)
```

profile of v0, /device:TPU:0, one launch (start us, length us, event | category | flops | bytes accessed | tf_op | source)
XLA Modules:
  0.0 40.9 jit_solution(16463728505834022918)
XLA Ops:
  0.0 0.0 copy-start
  0.0 0.0 copy-start.1
  0.0 1.0 %reshape.18 = bf16[4,48,48]{2,1,0:T(8,128)(2,1)S(1)} reshape(bf16[1,4,2304]{2,1,0:T(4,128)(2,1)} %param.3) | data formatting | bytes 36864 | tf_op jit(solution)/shard_map/reshape
  1.0 1.2 %convolution_bitcast_fusion = f32[4,48,48]{1,2,0:T(8,128)S(1)} fusion(bf16[4,48,48]{2,1,0:T(8,128)(2,1)S(1)} %reshape.18, f32[4,2,48,48]{3,2,1,0:T(8,128)} %param.5), kind=kOutput, calls=%fused_computation.3 | convolution fusion | flops 5308416 | bytes 153600 | tf_op jit(solution)/shard_map/mab,qmbc->qmac/dot_general | solution.py:15
  2.1 1.2 %fusion.3 = bf16[1,4,48,48]{3,2,1,0:T(8,128)(2,1)S(1)} fusion(f32[4,48,48]{1,2,0:T(8,128)S(1)} %convolution_bitcast_fusion, f32[4,2,48,48]{3,2,1,0:T(8,128)} %param.5), kind=kOutput, calls=%fused_computation.5 | convolution fusion | flops 5326848 | bytes 153600 | tf_op jit(solution)/shard_map/qmac,mcd->qmad/dot_general | solution.py:16
  3.4 0.1 reshape.20
  3.5 32.4 %all_gather.3 = bf16[8,4,2304]{2,1,0:T(4,128)(2,1)S(1)} all-gather(bf16[1,4,2304]{2,1,0:T(4,128)(2,1)S(1)} %reshape.20), channel_id=1, replica_groups=mesh['grp'=2,'rows'=8,'mod'=2] {'rows'}, dimensions={0}, use_global_device_ids=true | all-gather | bytes 165888 | tf_op jit(solution)/shard_map/all_gather | solution.py:27
  35.9 0.0 copy-done
  35.9 0.7 %fusion.4 = f32[8,128]{1,0:T(8,128)S(1)} fusion(bf16[128,4,2304]{2,1,0:T(4,128)(2,1)S(1)} %copy-done, bf16[8,4,2304]{2,1,0:T(4,128)(2,1)S(1)} %all_gather.3), kind=kOutput, calls=%fused_computation.6 | convolution fusion | flops 18874368 | bytes 2510848 | tf_op jit(solution)/shard_map/dot_general | solution.py:29
  36.6 2.5 %all-reduce = f32[8,128]{1,0:T(8,128)S(1)} all-reduce(f32[8,128]{1,0:T(8,128)S(1)} %fusion.4), channel_id=2, replica_groups=mesh['grp'=2,'rows'=8,'mod'=2] {'mod'}, use_global_device_ids=true, to_apply=%region_0.0.clone | all-reduce | flops 1024 | bytes 8192
  39.1 0.0 copy-done.1
  39.1 0.6 %dynamic-slice = u32[1]{0:T(128)} dynamic-slice(u32[32]{0:T(128)S(1)} %copy-done.1, u32[]{:T(128)S(6)} %add.3), dynamic_slice_sizes={1} | dynamic-slice | bytes 12
  40.3 0.6 %constant_dynamic-slice_fusion = f32[4,128]{1,0:T(4,128)} fusion(f32[8,128]{1,0:T(8,128)S(1)} %all-reduce, u32[]{:T(128)S(6)} %multiply.5), kind=kLoop, calls=%fused_computation.12 | loop fusion | bytes 4100
Async XLA Ops:
  0.0 35.9 %copy-start = (bf16[128,4,2304]{2,1,0:T(4,128)(2,1)S(1)}, bf16[128,4,2304]{2,1,0:T(4,128)(2,1)}, u32[]{:S(2)}) copy-start(bf16[128,4,2304]{2,1,0:T(4,128)(2,1)} %param.4) | copy-start | bytes 7077892
  0.0 39.1 %copy-start.1 = (u32[32]{0:T(128)S(1)}, u32[32]{0:T(128)}, u32[]{:S(2)}) copy-start(u32[32]{0:T(128)} %constant.6) | copy-start | bytes 388
where the time goes:
time: 41.1 us; the launch traced here: 40.9 us
  blocking collectives  34.8 us (85%)
  matrix products  3.1 us (8%)
  local copies, waits for them, and re-layouts  2.27 us (6%)
  between operations  0.68 us (2%)
    all_gather x1, blocking collectives, shards(): ready_rows = lax.all_gather(scaled_own, 'rows', axis=0, tiled=True)  32.4 us
    unnamed x1, blocking collectives  2.46 us
    dot_general x1, matrix products, precondition(): jnp.einsum('qmac,mcd->qmad', left_side, factors[:, 1], precision=lax.Prec...  1.24 us
    unnamed x6, local copies, waits for them, and re-layouts  1.18 us
    dot_general x1, matrix products, precondition(): jnp.einsum('mab,qmbc->qmac', factors[:, 0], grads, precision=lax.Precisio...  1.15 us
    reshape x1, local copies, waits for them, and re-layouts  0.98 us

commit v1 on v0

--- a/solution.py
+++ b/solution.py
@@ -6,6 +6,23 @@
 MODULES = 8
 PROJ = 48
 COORDS = 2304
+
+
+def in_order(tiles, dim):
+    tiles = jnp.moveaxis(tiles, 0, dim)
+    shape = tiles.shape
+    return tiles.reshape(*shape[:dim], shape[dim] * shape[dim + 1], *shape[dim + 2 :])
+
+
+def ring_gather(array, axis, dim):
+    peers = lax.axis_size(axis)
+    forward = [(i, (i + 1) % peers) for i in range(peers)]
+    blocks = [array]
+    while len(blocks) < peers:
+        blocks.append(lax.ppermute(blocks[-1], axis, forward))
+    place = lax.axis_index(axis)
+    blocks = jnp.stack(blocks)[(place - jnp.arange(peers)) % peers]
+    return in_order(blocks, dim)
 
 
 def precondition(grads_in, factors):
@@ -24,7 +41,7 @@
     train_count = train_grads.shape[0]
     train_flat = train_grads.reshape(train_count, -1)
     scaled_own = precondition(queries, factors)
-    ready_rows = lax.all_gather(scaled_own, "rows", axis=0, tiled=True)
+    ready_rows = ring_gather(scaled_own, "rows", 0)
     flat_rows = ready_rows.reshape(ready_rows.shape[0], -1)
     partial_value = lax.dot_general(
         flat_rows, train_flat, (((1,), (1,)), ((), ())), preferred_element_type=jnp.float32

time: 41.1 us -> 54.7 us (1.33)
  waiting for transfers between devices: 0 us -> 39.8 us
  blocking collectives: 34.8 us -> 2.47 us
  starting transfers between devices: 0 us -> 3.29 us
  local copies, waits for them, and re-layouts: 2.27 us -> 5.01 us
    ppermute x0 -> x7, waiting for transfers between devices: none -> 39.8 us  [ring_gather(): blocks.append(lax.ppermute(blocks[-1], axis, forward))]
    all_gather x1 -> x0, blocking collectives: 32.4 us -> none  [shards(): ready_rows = lax.all_gather(scaled_own, 'rows', axis=0, tiled=True)]
    ppermute x0 -> x7, starting transfers between devices: none -> 3.29 us  [ring_gather(): blocks.append(lax.ppermute(blocks[-1], axis, forward))]
    unnamed x6 -> x13, local copies, waits for them, and re-layouts: 1.18 us -> 3.27 us
    gather x0 -> x1, local copies, waits for them, and re-layouts: none -> 0.67 us  [ring_gather(): blocks = jnp.stack(blocks)[(place - jnp.arange(peers)) % peers]]
  transfers between devices with their start and end apart: 0 -> 7, of which waited for: 0 -> 7; matrix products, arithmetic and copies ran while one was open for 0% -> 5% of each run, Pallas kernels for 0% -> 0%
where the time goes in v1:
time: 54.7 us; the launch traced here: 54.4 us
  waiting for transfers between devices  39.8 us (73%)
  local copies, waits for them, and re-layouts  5.01 us (9%)
  starting transfers between devices  3.29 us (6%)
  matrix products  3.09 us (6%)
  blocking collectives  2.47 us (5%)
  between operations  0.78 us (1%)
    ppermute x7, waiting for transfers between devices, ring_gather(): blocks.append(lax.ppermute(blocks[-1], axis, forward))  39.8 us
    ppermute x7, starting transfers between devices, ring_gather(): blocks.append(lax.ppermute(blocks[-1], axis, forward))  3.29 us
    unnamed x13, local copies, waits for them, and re-layouts  3.27 us
    unnamed x1, blocking collectives  2.47 us
    dot_general x1, matrix products, precondition(): jnp.einsum('qmac,mcd->qmad', left_side, factors[:, 1], precision=lax.Prec...  1.24 us
    dot_general x1, matrix products, precondition(): jnp.einsum('mab,qmbc->qmac', factors[:, 0], grads, precision=lax.Precisio...  1.15 us
  transfers between devices with their start and end apart: 7, of which 7 were waited for; matrix products, arithmetic and copies ran while one was open for 5% of the time, Pallas kernels for 0%

profile of v1, /device:TPU:0, one launch (start us, length us, event | category | flops | bytes accessed | tf_op | source)
XLA Modules:
  0.0 54.4 jit_solution(12559932915170992699)
XLA Ops:
  0.0 0.8 %reshape.68 = bf16[4,48,48]{2,1,0:T(8,128)(2,1)S(1)} reshape(bf16[1,4,2304]{2,1,0:T(4,128)(2,1)} %param.3) | data formatting | bytes 36864 | tf_op jit(solution)/shard_map/reshape
  0.8 1.2 %convolution_bitcast_fusion = f32[4,48,48]{1,2,0:T(8,128)S(1)} fusion(bf16[4,48,48]{2,1,0:T(8,128)(2,1)S(1)} %reshape.68, f32[4,2,48,48]{3,2,1,0:T(8,128)} %param.5), kind=kOutput, calls=%fused_computation.2 | convolution fusion | flops 5308416 | bytes 153600 | tf_op jit(solution)/shard_map/mab,qmbc->qmac/dot_general | solution.py:32
  2.0 1.2 %fusion.1 = bf16[1,4,48,48]{3,2,1,0:T(8,128)(2,1)S(1)} fusion(f32[4,48,48]{1,2,0:T(8,128)S(1)} %convolution_bitcast_fusion, f32[4,2,48,48]{3,2,1,0:T(8,128)} %param.5), kind=kOutput, calls=%fused_computation.4 | convolution fusion | flops 5326848 | bytes 153600 | tf_op jit(solution)/shard_map/qmac,mcd->qmad/dot_general | solution.py:33
  3.2 0.1 reshape.70
  3.4 3.0 %collective-permute-start = (bf16[1,4,2304]{2,1,0:T(4,128)(2,1)S(1)}, bf16[1,4,2304]{2,1,0:T(4,128)(2,1)S(1)}, u32[]{:S(2)}, u32[]{:S(2)}) collective-permute-start(bf16[1,4,2304]{2,1,0:T(4,128)(2,1)S(1)} %reshape.70), channel_id=1, source_target_pairs={{0,2},{2,4},{4,6},{6,8},{8,10},{10,12},{12,14},{14,0},{1,3},{3,5},... | collective-permute-start | bytes 55304 | tf_op jit(solution)/shard_map/ppermute | solution.py:22
  6.4 0.1 stack_reshape.3
  6.6 0.0 copy-start
  6.6 2.0 %copy.17 = bf16[16,8,4,2304]{3,1,2,0:T(8,128)(2,1)S(1)} copy(bf16[16,8,4,2304]{3,2,1,0:T(4,128)(2,1)} %bitcast.53) | data formatting | bytes 4718592
  8.6 0.0 copy-done
  8.6 0.6 %dynamic-slice = u32[1]{0:T(128)} dynamic-slice(u32[32]{0:T(128)S(1)} %copy-done, u32[]{:T(128)S(6)} %add.28), dynamic_slice_sizes={1} | dynamic-slice | bytes 12
  9.8 1.4 %collective-permute-done = bf16[1,4,2304]{2,1,0:T(4,128)(2,1)S(1)} collective-permute-done((bf16[1,4,2304]{2,1,0:T(4,128)(2,1)S(1)}, bf16[1,4,2304]{2,1,0:T(4,128)(2,1)S(1)}, u32[]{:S(2)}, u32[]{:S(2)}) %collective-permute-start) | collective-permute-done | bytes 18464 | tf_op jit(solution)/shard_map/ppermute | solution.py:22
  11.2 0.3 collective-permute-start.1
  11.4 6.2 %collective-permute-done.1 = bf16[1,4,2304]{2,1,0:T(4,128)(2,1)S(1)} collective-permute-done((bf16[1,4,2304]{2,1,0:T(4,128)(2,1)S(1)}, bf16[1,4,2304]{2,1,0:T(4,128)(2,1)S(1)}, u32[]{:S(2)}, u32[]{:S(2)}) %collective-permute-start.1) | collective-permute-done | bytes 18464 | tf_op jit(solution)/shard_map/ppermute | solution.py:22
  17.6 0.0 collective-permute-start.2
  17.6 6.4 %collective-permute-done.2 = bf16[1,4,2304]{2,1,0:T(4,128)(2,1)S(1)} collective-permute-done((bf16[1,4,2304]{2,1,0:T(4,128)(2,1)S(1)}, bf16[1,4,2304]{2,1,0:T(4,128)(2,1)S(1)}, u32[]{:S(2)}, u32[]{:S(2)}) %collective-permute-start.2) | collective-permute-done | bytes 18464 | tf_op jit(solution)/shard_map/ppermute | solution.py:22
  24.1 0.0 collective-permute-start.3
  24.1 6.4 %collective-permute-done.3 = bf16[1,4,2304]{2,1,0:T(4,128)(2,1)S(1)} collective-permute-done((bf16[1,4,2304]{2,1,0:T(4,128)(2,1)S(1)}, bf16[1,4,2304]{2,1,0:T(4,128)(2,1)S(1)}, u32[]{:S(2)}, u32[]{:S(2)}) %collective-permute-start.3) | collective-permute-done | bytes 18464 | tf_op jit(solution)/shard_map/ppermute | solution.py:22
  30.5 0.0 collective-permute-start.4
  30.6 6.5 %collective-permute-done.4 = bf16[1,4,2304]{2,1,0:T(4,128)(2,1)S(1)} collective-permute-done((bf16[1,4,2304]{2,1,0:T(4,128)(2,1)S(1)}, bf16[1,4,2304]{2,1,0:T(4,128)(2,1)S(1)}, u32[]{:S(2)}, u32[]{:S(2)}) %collective-permute-start.4) | collective-permute-done | bytes 18464 | tf_op jit(solution)/shard_map/ppermute | solution.py:22
  37.0 0.0 collective-permute-start.5
  37.1 6.4 %collective-permute-done.5 = bf16[1,4,2304]{2,1,0:T(4,128)(2,1)S(1)} collective-permute-done((bf16[1,4,2304]{2,1,0:T(4,128)(2,1)S(1)}, bf16[1,4,2304]{2,1,0:T(4,128)(2,1)S(1)}, u32[]{:S(2)}, u32[]{:S(2)}) %collective-permute-start.5) | collective-permute-done | bytes 18464 | tf_op jit(solution)/shard_map/ppermute | solution.py:22
  43.5 0.0 collective-permute-start.6
  43.5 6.4 %collective-permute-done.6 = bf16[1,4,2304]{2,1,0:T(4,128)(2,1)S(1)} collective-permute-done((bf16[1,4,2304]{2,1,0:T(4,128)(2,1)S(1)}, bf16[1,4,2304]{2,1,0:T(4,128)(2,1)S(1)}, u32[]{:S(2)}, u32[]{:S(2)}) %collective-permute-start.6) | collective-permute-done | bytes 18464 | tf_op jit(solution)/shard_map/ppermute | solution.py:22
  50.0 0.7 %gather_fusion = bf16[8,4,2304]{2,1,0:T(4,128)(2,1)S(1)} fusion(bf16[8,4,2304]{2,1,0:T(4,128)(2,1)S(1)} %bitcast.56, s32[1024]{0:T(1024)S(1)} %pad_clamp_fusion), kind=kCustom, calls=%fused_computation | custom fusion | bytes 294944 | tf_op jit(solution)/shard_map/gather | solution.py:24
  50.7 0.7 %fusion.8 = f32[8,128]{1,0:T(8,128)S(1)} fusion(bf16[8,9216]{1,0:T(8,128)(2,1)S(1)} %bitcast.54, bf16[128,9216]{1,0:T(8,128)(2,1)S(1)} %bitcast.52), kind=kOutput, calls=%fused_computation.25 | convolution fusion | flops 18874368 | bytes 2510848 | tf_op jit(solution)/shard_map/dot_general | solution.py:46
  51.4 2.5 %all-reduce = f32[8,128]{1,0:T(8,128)S(1)} all-reduce(f32[8,128]{1,0:T(8,128)S(1)} %fusion.8), channel_id=2, replica_groups=mesh['grp'=2,'rows'=8,'mod'=2] {'mod'}, use_global_device_ids=true, to_apply=%region_0.1.clone | all-reduce | flops 1024 | bytes 8192
  53.9 0.6 %constant_dynamic-slice_fusion = f32[4,128]{1,0:T(4,128)} fusion(f32[8,128]{1,0:T(8,128)S(1)} %all-reduce, u32[]{:T(128)S(6)} %multiply.5), kind=kLoop, calls=%fused_computation.24 | loop fusion | bytes 4100
  (11 shorter events, 0.2 us)
Async XLA Ops:
  3.4 7.8 %collective-permute-start = (bf16[1,4,2304]{2,1,0:T(4,128)(2,1)S(1)}, bf16[1,4,2304]{2,1,0:T(4,128)(2,1)S(1)}, u32[]{:S(2)}, u32[]{:S(2)}) collective-permute-start(bf16[1,4,2304]{2,1,0:T(4,128)(2,1)S(1)} %reshape.70), channel_id=1, source_target_pairs={{0,2},{2,4},{4,6},{6,8},{8,10},{10,12},{12,14},{14,0},{1,3},{3,5},... | collective-permute-start | bytes 55304 | tf_op jit(solution)/shard_map/ppermute | solution.py:22
  6.6 2.0 %copy-start = (u32[32]{0:T(128)S(1)}, u32[32]{0:T(128)}, u32[]{:S(2)}) copy-start(u32[32]{0:T(128)} %constant.29) | copy-start | bytes 388
  11.2 6.5 %collective-permute-start.1 = (bf16[1,4,2304]{2,1,0:T(4,128)(2,1)S(1)}, bf16[1,4,2304]{2,1,0:T(4,128)(2,1)S(1)}, u32[]{:S(2)}, u32[]{:S(2)}) collective-permute-start(bf16[1,4,2304]{2,1,0:T(4,128)(2,1)S(1)} %collective-permute-done), channel_id=1, source_target_pairs={{0,2},{2,4},{4,6},{6,8},{8,10},{10,12},{12,14},{14,0},{1,3},{3,5},... | collective-permute-start | bytes 55304 | tf_op jit(solution)/shard_map/ppermute | solution.py:22
  17.6 6.5 %collective-permute-start.2 = (bf16[1,4,2304]{2,1,0:T(4,128)(2,1)S(1)}, bf16[1,4,2304]{2,1,0:T(4,128)(2,1)S(1)}, u32[]{:S(2)}, u32[]{:S(2)}) collective-permute-start(bf16[1,4,2304]{2,1,0:T(4,128)(2,1)S(1)} %collective-permute-done.1), channel_id=1, source_target_pairs={{0,2},{2,4},{4,6},{6,8},{8,10},{10,12},{12,14},{14,0},{1,3},{3,5},... | collective-permute-start | bytes 55304 | tf_op jit(solution)/shard_map/ppermute | solution.py:22
  24.1 6.5 %collective-permute-start.3 = (bf16[1,4,2304]{2,1,0:T(4,128)(2,1)S(1)}, bf16[1,4,2304]{2,1,0:T(4,128)(2,1)S(1)}, u32[]{:S(2)}, u32[]{:S(2)}) collective-permute-start(bf16[1,4,2304]{2,1,0:T(4,128)(2,1)S(1)} %collective-permute-done.2), channel_id=1, source_target_pairs={{0,2},{2,4},{4,6},{6,8},{8,10},{10,12},{12,14},{14,0},{1,3},{3,5},... | collective-permute-start | bytes 55304 | tf_op jit(solution)/shard_map/ppermute | solution.py:22
  30.5 6.5 %collective-permute-start.4 = (bf16[1,4,2304]{2,1,0:T(4,128)(2,1)S(1)}, bf16[1,4,2304]{2,1,0:T(4,128)(2,1)S(1)}, u32[]{:S(2)}, u32[]{:S(2)}) collective-permute-start(bf16[1,4,2304]{2,1,0:T(4,128)(2,1)S(1)} %collective-permute-done.3), channel_id=1, source_target_pairs={{0,2},{2,4},{4,6},{6,8},{8,10},{10,12},{12,14},{14,0},{1,3},{3,5},... | collective-permute-start | bytes 55304 | tf_op jit(solution)/shard_map/ppermute | solution.py:22
  37.0 6.5 %collective-permute-start.5 = (bf16[1,4,2304]{2,1,0:T(4,128)(2,1)S(1)}, bf16[1,4,2304]{2,1,0:T(4,128)(2,1)S(1)}, u32[]{:S(2)}, u32[]{:S(2)}) collective-permute-start(bf16[1,4,2304]{2,1,0:T(4,128)(2,1)S(1)} %collective-permute-done.4), channel_id=1, source_target_pairs={{0,2},{2,4},{4,6},{6,8},{8,10},{10,12},{12,14},{14,0},{1,3},{3,5},... | collective-permute-start | bytes 55304 | tf_op jit(solution)/shard_map/ppermute | solution.py:22
  43.5 6.5 %collective-permute-start.6 = (bf16[1,4,2304]{2,1,0:T(4,128)(2,1)S(1)}, bf16[1,4,2304]{2,1,0:T(4,128)(2,1)S(1)}, u32[]{:S(2)}, u32[]{:S(2)}) collective-permute-start(bf16[1,4,2304]{2,1,0:T(4,128)(2,1)S(1)} %collective-permute-done.5), channel_id=1, source_target_pairs={{0,2},{2,4},{4,6},{6,8},{8,10},{10,12},{12,14},{14,0},{1,3},{3,5},... | collective-permute-start | bytes 55304 | tf_op jit(solution)/shard_map/ppermute | solution.py:22
